TPU v7x, 256 devices: a whole 4x4x8 slice. The times are simulated.
256 devices in a mesh: req: 64 (over z, x, core), tp: 4 (over y).
Axes of the slice: x: 4, y: 4, z: 8, core: 2. Of those that a mesh axis runs over, the one named last changes fastest.
Arguments:
- tokens_new: bfloat16 [64, 16, 2, 1024], P('req'), may hold values from -6 to 6
- prefix_len: int32 [64], replicated, may hold values from 1 to 4096, as said below
- tail_len: int32 [64, 16], P('req'), may hold values from 1 to 512, as said below
- pool_home: int32 [2048], replicated, may hold values from 0 to 63, as said below
- pool_page: int32 [2048], replicated, may hold values from 0 to 31
- slot_page_cache: bfloat16 [2048, 128, 2, 512], P('req', None, None, 'tp'), may hold values from -64 to 64
- tail_cache: bfloat16 [64, 16, 512, 2, 512], P('req', None, None, None, 'tp'), may hold values from -6 to 6
- routes: int32 [64, 16, 2, 8], P('req'), may hold values from 0 to 31, all different within a row; in each aligned block of 32 rows (0 to 31, 32 to 63, ..., all dimensions but the last counted through in order) at most 12 rows name the same one
- norm_gains: float32 [3, 1024], replicated, may hold values from 0.1 to 1.9
- query_weight: bfloat16 [1024, 1024], P(None, 'tp'), may hold values from -0.1875 to 0.1875
- key_value_weight: bfloat16 [1024, 2, 512], P(None, None, 'tp'), may hold values from -0.1875 to 0.1875
- out_weight: bfloat16 [1024, 1024], P('tp'), may hold values from -0.1875 to 0.1875
- router: bfloat16 [1024, 32], replicated, may hold values from -0.375 to 0.375
- expert_in: bfloat16 [64, 1024, 2, 512], P('req', None, None, 'tp'), as said below
- expert_out: bfloat16 [64, 512, 1024], P('req', 'tp'), as said below
- score_weight: float32 [1024], replicated, may hold values from -0.1875 to 0.1875
Outputs:
- layer_out: bfloat16 [64, 16, 2, 1024], P('req')
- row_score: float32 [64, 16, 2], P('req')
Inputs may be any that keep to these rules, and one draw needn't show every extreme that they name: `prefix_len`: some request has exactly 4096 prefix positions. `tail_len`: some sample has exactly 512 tail positions. `pool_home`: entry s * 32 + v describes slot v of the pool of device s of req. Every page 0 to 31 of every request lies in exactly one slot, and one device's pool holds either exactly 1 pages of a request or none of them. `routes`: in the 32 rows of one device no expert is named more than 12 times. `expert_in`: expert table copy c equals copy c mod 32. `expert_out`: expert table copy c equals copy c mod 32.
All inputs are finite; a program needn't handle non-finite values.
Results may differ from a plain program's by a relative error of at most 0.017.
Values may be sent and summed in bfloat16 or wider, within the bound.
A program may use at most 128 MiB of HBM per device.

v0:
```python
import jax
import jax.numpy as jnp
from jax import lax
from jax.sharding import PartitionSpec as P

HEAD_DIM = 64
MOST = 12
EPSILON = 1e-05
ROPE_BASE = 10000.0
LOWEST = -1e30


def rms_scale(values, gain_row):
    widened = values.astype(jnp.float32)
    return (
        widened
        * lax.rsqrt(jnp.mean(widened * widened, axis=-1, keepdims=True) + EPSILON)
        * gain_row
    )


def apply_rotary(vectors, token_positions):
    half_width = vectors.shape[-1] // 2
    frequency = ROPE_BASE ** (-jnp.arange(half_width, dtype=jnp.float32) / half_width)
    angles = token_positions.astype(jnp.float32)[..., None] * frequency
    cosine = jnp.cos(angles)[..., None, :]
    sine_part = jnp.sin(angles)[..., None, :]
    leading = vectors[..., :half_width]
    trailing = vectors[..., half_width:]
    return jnp.concatenate(
        [leading * cosine - trailing * sine_part, trailing * cosine + leading * sine_part], axis=-1
    )


def block_stats(scores, visible):
    block_top = jnp.max(jnp.where(visible, scores, LOWEST), axis=-1)
    weights = jnp.where(
        visible, jnp.exp(jnp.where(visible, scores - block_top[..., None], 0.0)), 0.0
    )
    return (block_top, jnp.sum(weights, axis=-1), weights.astype(jnp.bfloat16))


def shards(
    tokens_new,
    prefix_len,
    tail_len,
    pool_home,
    pool_page,
    slot_page_cache,
    tail_cache,
    routes,
    norm_gains,
    query_weight,
    key_value_weight,
    out_weight,
    router,
    expert_in,
    expert_out,
    score_weight,
):
    device = lax.axis_index("req")
    req_count = lax.axis_size("req")
    samples = tokens_new.shape[1]
    fresh_count = tokens_new.shape[2]
    model_width = tokens_new.shape[3]
    row_count = samples * fresh_count
    head_count = query_weight.shape[1] // HEAD_DIM
    kv_heads = key_value_weight.shape[2] // HEAD_DIM
    query_group_width = head_count // kv_heads
    pool_slots = slot_page_cache.shape[0]
    page_size = slot_page_cache.shape[1]
    slot_cap = max(1, pool_slots // req_count)
    score_scale = HEAD_DIM ** (-0.5)
    flat_tokens = tokens_new.reshape(row_count, model_width)
    normalized_input = rms_scale(flat_tokens, norm_gains[0]).astype(jnp.bfloat16)
    query_vectors = jnp.dot(
        normalized_input, query_weight, preferred_element_type=jnp.float32
    ).reshape(samples, fresh_count, head_count, HEAD_DIM)
    key_value_rows = jnp.dot(
        normalized_input,
        key_value_weight.reshape(model_width, 2 * kv_heads * HEAD_DIM),
        preferred_element_type=jnp.float32,
    ).reshape(samples, fresh_count, 2, kv_heads, HEAD_DIM)
    own_length = jnp.take(prefix_len, device)
    token_positions = (
        own_length + tail_len[0][:, None] + jnp.arange(fresh_count, dtype=jnp.int32)[None, :]
    )
    rotated_query = (
        apply_rotary(query_vectors, token_positions)
        .astype(jnp.bfloat16)
        .reshape(samples, fresh_count, kv_heads, query_group_width, HEAD_DIM)
    )
    key_rot = apply_rotary(key_value_rows[:, :, 0], token_positions).astype(jnp.bfloat16)
    value_new = key_value_rows[:, :, 1].astype(jnp.bfloat16)
    owner_homes = pool_home.reshape(req_count, pool_slots)
    owner_pages = pool_page.reshape(req_count, pool_slots)
    own_home = jnp.take(owner_homes, device, axis=0)
    slot_range = jnp.arange(pool_slots, dtype=jnp.int32)
    cap_range = jnp.arange(slot_cap, dtype=jnp.int32)
    same_home = own_home[:, None] == own_home[None, :]
    earlier = slot_range[:, None] <= slot_range[None, :]
    slot_rank = jnp.sum((same_home & earlier).astype(jnp.int32), axis=0)
    picked_slots = (
        own_home[None, None, :] == jnp.arange(req_count, dtype=jnp.int32)[:, None, None]
    ) & (slot_rank[None, None, :] == cap_range[None, :, None] + 1)
    slot_index = jnp.sum(
        picked_slots.astype(jnp.int32) * slot_range[None, None, :], axis=-1
    ).reshape(-1)
    page_range = jnp.arange(page_size, dtype=jnp.int32)
    outgoing = jnp.take(slot_page_cache, slot_index, axis=0).reshape(
        (req_count, slot_cap) + slot_page_cache.shape[1:]
    )
    arrived = lax.all_to_all(outgoing, "req", split_axis=0, concat_axis=0, tiled=True)
    home_match = owner_homes == device
    home_rank = jnp.cumsum(home_match.astype(jnp.int32), axis=1)
    wanted = home_match[:, None, :] & (home_rank[:, None, :] == cap_range[None, :, None] + 1)
    page_ids = jnp.where(
        jnp.any(wanted, axis=-1),
        jnp.sum(wanted.astype(jnp.int32) * owner_pages[:, None, :], axis=-1),
        -1,
    ).reshape(-1)
    blocks = arrived.reshape(req_count * slot_cap, page_size, 2, kv_heads, HEAD_DIM)
    page_scores = (
        jnp.einsum(
            "sikgd,btkd->bsikgt", rotated_query, blocks[:, :, 0], preferred_element_type=jnp.float32
        )
        * score_scale
    )
    page_spots = page_ids[:, None] * page_size + page_range[None, :]
    page_seen = ((page_spots < own_length) & (page_ids[:, None] >= 0))[:, None, None, None, None, :]
    page_top, page_total, page_weights = block_stats(page_scores, page_seen)
    page_numer = jnp.einsum(
        "bsikgt,btkd->bsikgd", page_weights, blocks[:, :, 1], preferred_element_type=jnp.float32
    )
    tail_count = tail_cache.shape[2]
    tail_block_list = tail_cache[0].reshape(
        samples, tail_count // page_size, page_size, 2, kv_heads, HEAD_DIM
    )
    tail_scores = (
        jnp.einsum(
            "sikgd,sbtkd->sbikgt",
            rotated_query,
            tail_block_list[:, :, :, 0],
            preferred_element_type=jnp.float32,
        )
        * score_scale
    )
    tail_spots = jnp.arange(tail_count, dtype=jnp.int32).reshape(tail_count // page_size, page_size)
    tail_seen = (tail_spots[None] < tail_len[0][:, None, None])[:, :, None, None, None, :]
    tail_top, tail_total, tail_weights = block_stats(tail_scores, tail_seen)
    tail_numer = jnp.einsum(
        "sbikgt,sbtkd->sbikgd",
        tail_weights,
        tail_block_list[:, :, :, 1],
        preferred_element_type=jnp.float32,
    )
    fresh_scores = (
        jnp.einsum("sikgd,sjkd->sikgj", rotated_query, key_rot, preferred_element_type=jnp.float32)
        * score_scale
    )
    fresh_range = jnp.arange(fresh_count, dtype=jnp.int32)
    fresh_seen = (fresh_range[None, :] <= fresh_range[:, None])[None, :, None, None, :]
    fresh_top, fresh_total, fresh_weights = block_stats(fresh_scores, fresh_seen)
    fresh_numer = jnp.einsum(
        "sikgj,sjkd->sikgd", fresh_weights, value_new, preferred_element_type=jnp.float32
    )
    overall = jnp.maximum(
        jnp.maximum(jnp.max(page_top, axis=0), jnp.max(tail_top, axis=1)), fresh_top
    )
    page_factor = jnp.exp(page_top - overall[None])
    tail_factor = jnp.exp(tail_top - overall[:, None])
    fresh_factor = jnp.exp(fresh_top - overall)
    denominator = (
        jnp.sum(page_factor * page_total, axis=0)
        + jnp.sum(tail_factor * tail_total, axis=1)
        + fresh_factor * fresh_total
    )
    numerator = (
        jnp.sum(page_factor[..., None] * page_numer, axis=0)
        + jnp.sum(tail_factor[..., None] * tail_numer, axis=1)
        + fresh_factor[..., None] * fresh_numer
    )
    attn_rows = (
        (numerator / denominator[..., None])
        .astype(jnp.bfloat16)
        .reshape(row_count, head_count * HEAD_DIM)
    )
    attn_part = jnp.dot(attn_rows, out_weight, preferred_element_type=jnp.float32)
    attn_out = lax.psum(attn_part, "tp")
    residual = (flat_tokens.astype(jnp.float32) + attn_out).astype(jnp.bfloat16)
    normed_moe = rms_scale(residual, norm_gains[1]).astype(jnp.bfloat16)
    logits = jnp.dot(normed_moe, router, preferred_element_type=jnp.float32)
    routing = routes.reshape(row_count, -1)
    top_count = routing.shape[1]
    expert_count = router.shape[1]
    expert_range = jnp.arange(expert_count, dtype=jnp.int32)
    route_table = (routing[:, :, None] == expert_range[None, None, :]).astype(jnp.float32)
    picked = jnp.sum(route_table * logits[:, None, :], axis=-1)
    gate_values = jax.nn.softmax(picked, axis=-1)
    local_experts = expert_in.shape[0]
    copies = local_experts * req_count // expert_count
    expert_slot = routing + expert_count * (device % copies)
    onehot = (routing.reshape(-1)[:, None] == expert_range[None, :]).astype(jnp.int32)
    arrival = jnp.sum(jnp.cumsum(onehot, axis=0) * onehot, axis=1) - 1
    target = (expert_slot.reshape(-1) * MOST + arrival).reshape(row_count, top_count)
    buffer = req_count * local_experts * MOST
    hits = (target[None, :, :] == jnp.arange(buffer, dtype=jnp.int32)[:, None, None]).astype(
        jnp.float32
    )
    spread = jnp.sum(hits, axis=-1).astype(jnp.bfloat16)
    combine = jnp.transpose(jnp.sum(hits * gate_values[None], axis=-1))
    outgoing_rows = (
        jnp.dot(spread, normed_moe, preferred_element_type=jnp.float32)
        .astype(jnp.bfloat16)
        .reshape(req_count, local_experts, MOST, model_width)
    )
    gate_up = jnp.einsum(
        "necd,edgf->necgf",
        lax.all_to_all(outgoing_rows, "req", split_axis=0, concat_axis=0, tiled=True),
        expert_in,
        preferred_element_type=jnp.float32,
    )
    hidden = (jax.nn.silu(gate_up[:, :, :, 0]) * gate_up[:, :, :, 1]).astype(jnp.bfloat16)
    result = jnp.einsum("necf,efd->necd", hidden, expert_out, preferred_element_type=jnp.float32)
    returned = lax.all_to_all(
        result.astype(jnp.bfloat16), "req", split_axis=0, concat_axis=0, tiled=True
    ).astype(result.dtype)
    mixed_part = jnp.dot(combine, returned.reshape(buffer, -1), precision=lax.Precision.HIGHEST)
    expert_mix = lax.psum(mixed_part.astype(jnp.bfloat16), "tp").astype(jnp.float32)
    layer_out = (residual.astype(jnp.float32) + expert_mix).astype(jnp.bfloat16)
    final_norm = rms_scale(layer_out, norm_gains[2])
    row_score = jnp.sum(final_norm * score_weight, axis=-1)
    return (
        layer_out.reshape(1, samples, fresh_count, model_width),
        row_score.reshape(1, samples, fresh_count),
    )


def solution(mesh):
    placed = (
        P("req", None, None, None),
        P(),
        P("req", None),
        P(),
        P(),
        P("req", None, None, "tp"),
        P("req", None, None, None, "tp"),
        P("req", None, None, None),
        P(),
        P(None, "tp"),
        P(None, None, "tp"),
        P("tp", None),
        P(),
        P("req", None, None, "tp"),
        P("req", "tp", None),
        P(),
    )
    return jax.shard_map(
        shards,
        mesh=mesh,
        in_specs=placed,
        out_specs=(P("req", None, None, None), P("req", None, None)),
        check_vma=False,
    )
```

profile of v0, /device:TPU:2, one launch (start us, length us, event | category | flops | bytes accessed | tf_op | source)
XLA Modules:
  0.0 399.7 jit_solution(14285597943707223789)
XLA Ops:
  7.2 0.9 reshape.516
  8.4 0.4 copy-done
  8.8 10.7 %gather_fusion = bf16[64,128,2,128]{3,2,1,0:T(2,128)(2,1)} fusion(bf16[32,128,2,128]{3,2,1,0:T(2,128)(2,1)S(1)} %copy-done, s32[1024]{0:T(1024)S(1)} %pad_clamp_fusion), kind=kCustom, calls=%fused_computation | custom fusion | bytes 8388864 | tf_op jit(solution)/shard_map/jit(_take)/gather | solution.py:110
  19.5 7.9 %fusion.4 = bf16[64,1,128,2,128]{4,3,2,1,0:T(2,128)(2,1)} fusion(bf16[64,128,2,128]{3,2,1,0:T(2,128)(2,1)} %gather_fusion, pred[64]{0:T(512)(128)(4,1)S(1)} %compare_and_fusion), kind=kLoop, calls=%fused_computation.9 | loop fusion | flops 2097152 | bytes 8388672 | tf_op jit(solution)/shard_map/jit(_take)/select_n | solution.py:110
  27.4 12.3 %all-to-all-start = ((bf16[64,1,128,2,128]{4,3,2,1,0:T(2,128)(2,1)}), bf16[64,1,128,2,128]{4,3,2,1,0:T(2,128)(2,1)}, u32[]{:S(2)}, u32[]{:S(2)}) async-start(bf16[64,1,128,2,128]{4,3,2,1,0:T(2,128)(2,1)} %fusion.4), calls=%async_computation | async-start | bytes 8388608 | tf_op jit(solution)/shard_map/all_to_all | solution.py:113
  39.7 0.2 all-reduce.3.cloned.1.call-start
  40.2 0.6 dynamic-slice.5
  40.8 0.2 copy.276
  41.1 0.2 reduce_window_sum.26
  41.4 11.1 %copy.280 = bf16[1,16,512,2,128]{2,4,3,1,0:T(8,128)(2,1)} copy(bf16[1,16,512,2,128]{4,3,2,1,0:T(2,128)(2,1)} %param.22) | data formatting | bytes 8388608 | tf_op args[6]
  52.6 6.9 %reshape_squeeze.3 = bf16[16,4,128,2,2,64]{2,1,5,4,3,0:T(4,128)(2,1)} reshape(bf16[1,16,512,2,128]{2,4,3,1,0:T(8,128)(2,1)} %copy.280) | data formatting | bytes 8388608 | tf_op jit(solution)/shard_map/reshape;squeeze | solution.py:136
  60.2 0.1 multiply_reduce_fusion.2
  60.4 0.6 fusion.86
  61.0 0.1 multiply_cosine_fusion
  61.2 0.1 fusion.79
  61.3 0.3 fusion.47
  61.9 5.0 %fusion.85 = (bf16[16,4,128,1,2,64]{2,1,5,4,3,0:T(4,128)(2,1)S(1)}, bf16[16,4,128,1,2,64]{2,1,5,4,3,0:T(4,128)(2,1)}) fusion(bf16[16,4,128,2,2,64]{2,1,5,4,3,0:T(4,128)(2,1)} %reshape_squeeze.3), kind=kLoop, calls=%fused_computation.163 | loop fusion | bytes 8388608 | tf_op jit(solution)/shard_map/slice | solution.py:143
  67.0 0.6 fusion.31
  67.6 1.0 fusion.80
  68.6 0.7 copy.283
  69.4 0.2 copy.284
  69.6 0.3 fusion.45
  70.2 0.7 fusion.58
  70.9 0.2 copy.288
  71.1 0.7 fusion.83
  71.8 0.1 copy.304
  72.0 0.6 reduce-window.6
  72.6 0.2 slice_reduce_fusion
  73.0 0.1 select_reduce_fusion.3
  73.1 0.1 reduce_or.9
  73.4 0.2 fusion.65
  73.5 62.3 %all-to-all-done = bf16[64,1,128,2,128]{4,3,2,1,0:T(2,128)(2,1)} async-done(((bf16[64,1,128,2,128]{4,3,2,1,0:T(2,128)(2,1)}), bf16[64,1,128,2,128]{4,3,2,1,0:T(2,128)(2,1)}, u32[]{:S(2)}, u32[]{:S(2)}) %all-to-all-start) | async-done | bytes 4194336 | tf_op jit(solution)/shard_map/all_to_all | solution.py:113
  135.8 10.9 %copy.272 = bf16[64,1,128,2,128]{2,4,3,0,1:T(8,128)(2,1)} copy(bf16[64,1,128,2,128]{4,3,2,1,0:T(2,128)(2,1)} %all-to-all-done) | data formatting | bytes 8388608 | tf_op jit(solution)/shard_map/all_to_all | solution.py:113
  146.8 3.1 fusion.6
  149.9 3.3 fusion.7
  153.3 0.3 multiply_reduce_fusion
  153.5 0.2 multiply_reduce_fusion.1
  153.8 0.7 fusion.72
  154.5 11.1 %copy.345 = bf16[64,1,128,2,128]{2,4,0,3,1:T(8,128)(2,1)} copy(bf16[64,1,128,2,128]{4,3,2,1,0:T(2,128)(2,1)} %all-to-all-done) | data formatting | bytes 8388608 | tf_op jit(solution)/shard_map/reshape | solution.py:122
  165.7 3.0 fusion
  168.7 1.3 fusion.24
  170.0 0.1 fusion.44
  170.2 0.9 fusion.87
  171.1 0.3 all-reduce.5.cloned.1.call-start
  171.4 42.5 %all-reduce.3.cloned.1.call-done = f32[32,1024]{1,0:T(8,128)} async-done(((f32[32,1024]{1,0:T(8,128)}), f32[32,1024]{1,0:T(8,128)}) %all-reduce.3.cloned.1.call-update) | async-done | bytes 131088 | tf_op jit(solution)/shard_map/psum | solution.py:189
  213.9 1.0 fusion.37
  215.0 0.2 fusion.61
  215.2 0.2 select_reduce_fusion.1
  215.4 0.1 reduce_max.59
  215.7 0.6 convert_reduce_fusion
  216.3 1.8 convolution_convert_fusion
  218.0 2.4 reshape.522
  220.5 61.7 %all_to_all.15 = bf16[64,1,12,1024]{3,2,1,0:T(8,128)(2,1)S(1)} all-to-all(bf16[64,1,12,1024]{3,2,1,0:T(8,128)(2,1)S(1)} %bitcast.214), channel_id=1, replica_groups=mesh['req'=64,'tp'=4] {'req'}, dimensions={0} | all-to-all | bytes 3145728 | tf_op jit(solution)/shard_map/all_to_all | solution.py:219
  282.2 1.8 fusion.17
  284.0 0.6 fusion.16
  284.6 0.9 copy.321
  285.5 56.7 %all_to_all.16 = bf16[64,1,12,1024]{3,2,1,0:T(8,128)(2,1)} all-to-all(bf16[64,1,12,1024]{3,2,1,0:T(8,128)(2,1)S(1)} %copy.321), channel_id=1, replica_groups=mesh['req'=64,'tp'=4] {'req'}, dimensions={0} | all-to-all | bytes 3145728 | tf_op jit(solution)/shard_map/all_to_all | solution.py:225
  342.2 3.6 reshape.526
  345.9 2.9 convolution_convert_fusion.2
  348.8 41.5 %all-reduce.5.cloned.1.call-done = bf16[32,1024]{1,0:T(8,128)(2,1)} async-done(((bf16[32,1024]{1,0:T(8,128)(2,1)}), bf16[32,1024]{1,0:T(8,128)(2,1)}) %all-reduce.5.cloned.1.call-update) | async-done | bytes 65552 | tf_op jit(solution)/shard_map/psum | solution.py:229
  390.3 1.0 fusion.33
  391.2 0.7 reshape.527
  391.9 0.2 fusion.36
  392.2 0.7 copy.322
  (93 shorter events, 2.6 us)
Async XLA Ops:
  7.2 1.6 copy-start
  27.4 12.6 %copy-start.12 = (s32[1,16,2,8]{1,3,2,0:T(8,128)S(1)}, s32[1,16,2,8]{1,3,2,0:T(8,128)}, u32[]{:S(2)}) copy-start(s32[1,16,2,8]{1,3,2,0:T(8,128)} %param.23) | copy-start | bytes 3076
  27.4 12.9 %copy-start.18 = (s32[64]{0:T(128)S(1)}, s32[64]{0:T(128)}, u32[]{:S(2)}) copy-start(s32[64]{0:T(128)} %param.17) | copy-start | bytes 772
  27.4 13.5 %copy-start.4 = (bf16[1024,256]{1,0:T(8,128)(2,1)S(1)}, bf16[1024,256]{1,0:T(8,128)(2,1)}, u32[]{:S(2)}) copy-start(bf16[1024,256]{1,0:T(8,128)(2,1)} %param.25) | copy-start | bytes 1572868
  27.4 13.9 %copy-start.8 = (s32[2048]{0:T(1024)S(1)}, s32[2048]{0:T(1024)}, u32[]{:S(2)}) copy-start(s32[2048]{0:T(1024)} %param.19) | copy-start | bytes 24580
  27.4 14.0 %copy-start.13 = (s32[2048]{0:T(1024)S(1)}, s32[2048]{0:T(1024)}, u32[]{:S(2)}) copy-start(s32[2048]{0:T(1024)} %param.20) | copy-start | bytes 24580
  27.4 108.5 %all-to-all-start = ((bf16[64,1,128,2,128]{4,3,2,1,0:T(2,128)(2,1)}), bf16[64,1,128,2,128]{4,3,2,1,0:T(2,128)(2,1)}, u32[]{:S(2)}, u32[]{:S(2)}) async-start(bf16[64,1,128,2,128]{4,3,2,1,0:T(2,128)(2,1)} %fusion.4), calls=%async_computation | async-start | bytes 8388608 | tf_op jit(solution)/shard_map/all_to_all | solution.py:113
  39.7 174.2 %all-reduce.3.cloned.1.call-start = ((), (), s32[]{:S(2)}) async-start(), calls=%async_computation.3 | async-start | bytes 262144 | tf_op jit(solution)/shard_map/psum | solution.py:189
  52.6 7.0 %copy-start.3 = (bf16[1,16,2,1024]{3,2,1,0:T(2,128)(2,1)S(1)}, bf16[1,16,2,1024]{3,2,1,0:T(2,128)(2,1)}, u32[]{:S(2)}) copy-start(bf16[1,16,2,1024]{3,2,1,0:T(2,128)(2,1)} %param.16) | copy-start | bytes 196612
  52.6 7.8 %copy-start.15 = (s32[1,16]{1,0:T(1,128)S(1)}, s32[1,16]{1,0:T(1,128)}, u32[]{:S(2)}) copy-start(s32[1,16]{1,0:T(1,128)} %param.18) | copy-start | bytes 196
  52.6 7.8 %copy-start.11 = (f32[3,1024]{1,0:T(4,128)S(1)}, f32[3,1024]{1,0:T(4,128)}, u32[]{:S(2)}) copy-start(f32[3,1024]{1,0:T(4,128)} %param.24) | copy-start | bytes 36868
  67.0 2.3 copy-start.5
  149.8 3.3 copy-start.10
  165.7 3.0 copy-start.2
  168.7 1.6 copy-start.6
  168.7 46.3 %copy-start.17 = (bf16[1024,32]{0,1:T(8,128)(2,1)S(1)}, bf16[1024,32]{0,1:T(8,128)(2,1)}, u32[]{:S(2)}) copy-start(bf16[1024,32]{0,1:T(8,128)(2,1)} %param.28) | copy-start | bytes 196612
  171.1 219.2 %all-reduce.5.cloned.1.call-start = ((), (), s32[]{:S(2)}) async-start(), calls=%async_computation.4 | async-start | bytes 131072 | tf_op jit(solution)/shard_map/psum | solution.py:229
  218.0 64.2 %copy-start.16 = (bf16[1,1024,2,128]{3,2,1,0:T(2,128)(2,1)S(1)}, bf16[1,1024,2,128]{3,2,1,0:T(2,128)(2,1)}, u32[]{:S(2)}) copy-start(bf16[1,1024,2,128]{3,2,1,0:T(2,128)(2,1)} %param.29) | copy-start | bytes 1572868
  220.5 63.5 %copy-start.7 = (bf16[1,128,1024]{2,1,0:T(8,128)(2,1)S(1)}, bf16[1,128,1024]{2,1,0:T(8,128)(2,1)}, u32[]{:S(2)}) copy-start(bf16[1,128,1024]{2,1,0:T(8,128)(2,1)} %param.30) | copy-start | bytes 786436
  285.5 107.3 %copy-start.1 = (bf16[32,128,2,128]{3,2,1,0:T(2,128)(2,1)S(1)}, bf16[32,128,2,128]{3,2,1,0:T(2,128)(2,1)}, u32[]{:S(2)}) copy-start(bf16[32,128,2,128]{3,2,1,0:T(2,128)(2,1)} %param.21) | copy-start | bytes 6291460
  342.2 49.7 %copy-start.9 = (f32[1,1024]{1,0:T(1,128)S(1)}, f32[1,1024]{1,0:T(1,128)}, u32[]{:S(2)}) copy-start(f32[1,1024]{1,0:T(1,128)} %get-tuple-element.70) | copy-start | bytes 12292
  342.2 49.7 %copy-start.14 = (f32[1024]{0:T(1024)S(1)}, f32[1024]{0:T(1024)}, u32[]{:S(2)}) copy-start(f32[1024]{0:T(1024)} %param.31) | copy-start | bytes 12292
Sparse Core Ops, SparseCore 0:
  171.2 42.6 all-reduce.2
  348.9 41.2 all-reduce.4
where the time goes:
time: 401 us; the launch traced here: 400 us
  waiting for transfers between devices  146 us (36%)
  blocking collectives  118 us (29%)
  local copies, waits for them, and re-layouts  69.6 us (17%)
  other arithmetic  19.8 us (5%)
  matrix products  17.5 us (4%)
  between operations  15.2 us (4%)
  starting transfers between devices  12.8 us (3%)
    all_to_all x1, waiting for transfers between devices, shards(): lax.all_to_all(outgoing, 'req', split_axis=0, concat_axis=0, tiled=True)  62.3 us
    all_to_all x1, blocking collectives, shards(): lax.all_to_all(outgoing_rows, 'req', split_axis=0, concat_axis=0, tiled=T...  61.7 us
    all_to_all x1, blocking collectives, shards(): lax.all_to_all(result.astype(jnp.bfloat16), 'req', split_axis=0, concat_a...  56.7 us
    psum x1, waiting for transfers between devices, shards(): attn_out = lax.psum(attn_part, 'tp')  42.5 us
    psum x1, waiting for transfers between devices, shards(): lax.psum(mixed_part.astype(jnp.bfloat16), 'tp').astype(jnp.float32)  41.5 us
    unnamed x43, local copies, waits for them, and re-layouts  12.7 us
    all_to_all x1, starting transfers between devices, shards(): lax.all_to_all(outgoing, 'req', split_axis=0, concat_axis=0, tiled=True)  12.3 us
    reshape x1, local copies, waits for them, and re-layouts, shards(): arrived.reshape(req_count * slot_cap, page_size, 2, kv_heads, HEAD_DIM)  11.1 us
  transfers between devices with their start and end apart: 3, of which 3 were waited for; matrix products, arithmetic and copies ran while one was open for 8% of the time, Pallas kernels for 0%

commit v1 on v0

--- a/solution.py
+++ b/solution.py
@@ -186,7 +186,9 @@
         .reshape(row_count, head_count * HEAD_DIM)
     )
     attn_part = jnp.dot(attn_rows, out_weight, preferred_element_type=jnp.float32)
-    attn_out = lax.psum(attn_part, "tp")
+    attn_out = attn_part
+    for hop in (1, 2):
+        attn_out = attn_out + lax.ppermute(attn_out, "tp", [(dev, dev ^ hop) for dev in range(4)])
     residual = (flat_tokens.astype(jnp.float32) + attn_out).astype(jnp.bfloat16)
     normed_moe = rms_scale(residual, norm_gains[1]).astype(jnp.bfloat16)
     logits = jnp.dot(normed_moe, router, preferred_element_type=jnp.float32)

time: 401 us -> 365 us (0.910)
  waiting for transfers between devices: 146 us -> 114 us
  starting transfers between devices: 12.8 us -> 17.7 us
    psum x1 -> x0, waiting for transfers between devices: 42.5 us -> none  [shards(): attn_out = lax.psum(attn_part, 'tp')]
    ppermute x0 -> x2, waiting for transfers between devices: none -> 6.54 us  [shards(): lax.ppermute(attn_out, 'tp', [(dev, dev ^ hop) for dev in range(4)])]
    ppermute x0 -> x2, starting transfers between devices: none -> 5.18 us  [shards(): lax.ppermute(attn_out, 'tp', [(dev, dev ^ hop) for dev in range(4)])]
    all_to_all x1, blocking collectives: 61.7 us -> 57.3 us  [shards(): lax.all_to_all(outgoing_rows, 'req', split_axis=0, concat_axis=0, tiled=T...]
    unnamed x43 -> x39, local copies, waits for them, and re-layouts: 12.7 us -> 12.7 us
  transfers between devices with their start and end apart: 3 -> 4, of which waited for: 3 -> 4; matrix products, arithmetic and copies ran while one was open for 8% -> 9% of each run, Pallas kernels for 0% -> 0%
where the time goes in v1:
time: 365 us; the launch traced here: 363 us
  waiting for transfers between devices  114 us (31%)
  blocking collectives  114 us (31%)
  local copies, waits for them, and re-layouts  68.4 us (19%)
  starting transfers between devices  17.7 us (5%)
  other arithmetic  17.6 us (5%)
  matrix products  16.9 us (5%)
  between operations  15.2 us (4%)
    all_to_all x1, waiting for transfers between devices, shards(): lax.all_to_all(outgoing, 'req', split_axis=0, concat_axis=0, tiled=True)  64.2 us
    all_to_all x1, blocking collectives, shards(): lax.all_to_all(outgoing_rows, 'req', split_axis=0, concat_axis=0, tiled=T...  57.3 us
    all_to_all x1, blocking collectives, shards(): lax.all_to_all(result.astype(jnp.bfloat16), 'req', split_axis=0, concat_a...  56.7 us
    psum x1, waiting for transfers between devices, shards(): lax.psum(mixed_part.astype(jnp.bfloat16), 'tp').astype(jnp.float32)  43 us
    unnamed x39, local copies, waits for them, and re-layouts  12.7 us
    all_to_all x1, starting transfers between devices, shards(): lax.all_to_all(outgoing, 'req', split_axis=0, concat_axis=0, tiled=True)  12.3 us
    reshape x1, local copies, waits for them, and re-layouts, shards(): arrived.reshape(req_count * slot_cap, page_size, 2, kv_heads, HEAD_DIM)  11.1 us
    all_to_all x1, local copies, waits for them, and re-layouts, shards(): lax.all_to_all(outgoing, 'req', split_axis=0, concat_axis=0, tiled=True)  10.9 us
  transfers between devices with their start and end apart: 4, of which 4 were waited for; matrix products, arithmetic and copies ran while one was open for 9% of the time, Pallas kernels for 0%

profile of v1, /device:TPU:2, one launch (start us, length us, event | category | flops | bytes accessed | tf_op | source)
XLA Modules:
  0.0 363.4 jit_solution(620903256921395651)
XLA Ops:
  7.2 0.9 reshape.516
  8.2 0.1 select_reduce_fusion.2
  8.4 0.4 copy-done
  8.8 10.7 %gather_fusion = bf16[64,128,2,128]{3,2,1,0:T(2,128)(2,1)} fusion(bf16[32,128,2,128]{3,2,1,0:T(2,128)(2,1)S(1)} %copy-done, s32[1024]{0:T(1024)S(1)} %pad_clamp_fusion), kind=kCustom, calls=%fused_computation | custom fusion | bytes 8388864 | tf_op jit(solution)/shard_map/jit(_take)/gather | solution.py:110
  19.5 7.9 %fusion.4 = bf16[64,1,128,2,128]{4,3,2,1,0:T(2,128)(2,1)} fusion(bf16[64,128,2,128]{3,2,1,0:T(2,128)(2,1)} %gather_fusion, pred[64]{0:T(512)(128)(4,1)S(1)} %compare_and_fusion), kind=kLoop, calls=%fused_computation.9 | loop fusion | flops 2097152 | bytes 8388672 | tf_op jit(solution)/shard_map/jit(_take)/select_n | solution.py:110
  27.4 12.3 %all-to-all-start = ((bf16[64,1,128,2,128]{4,3,2,1,0:T(2,128)(2,1)}), bf16[64,1,128,2,128]{4,3,2,1,0:T(2,128)(2,1)}, u32[]{:S(2)}, u32[]{:S(2)}) async-start(bf16[64,1,128,2,128]{4,3,2,1,0:T(2,128)(2,1)} %fusion.4), calls=%async_computation | async-start | bytes 8388608 | tf_op jit(solution)/shard_map/all_to_all | solution.py:113
  39.7 0.2 all-reduce.2.cloned.1.call-start
  40.2 0.6 dynamic-slice.5
  40.8 0.2 copy.276
  41.1 0.2 reduce_window_sum.26
  41.4 11.1 %copy.280 = bf16[1,16,512,2,128]{2,4,3,1,0:T(8,128)(2,1)} copy(bf16[1,16,512,2,128]{4,3,2,1,0:T(2,128)(2,1)} %param.22) | data formatting | bytes 8388608 | tf_op args[6]
  52.6 6.9 %reshape_squeeze.3 = bf16[16,4,128,2,2,64]{2,1,5,4,3,0:T(4,128)(2,1)} reshape(bf16[1,16,512,2,128]{2,4,3,1,0:T(8,128)(2,1)} %copy.280) | data formatting | bytes 8388608 | tf_op jit(solution)/shard_map/reshape;squeeze | solution.py:136
  60.2 0.1 multiply_reduce_fusion.2
  60.4 0.1 multiply_cosine_fusion
  60.6 0.1 fusion.79
  60.7 0.3 fusion.47
  61.4 5.0 %fusion.85 = (bf16[16,4,128,1,2,64]{2,1,5,4,3,0:T(4,128)(2,1)S(1)}, bf16[16,4,128,1,2,64]{2,1,5,4,3,0:T(4,128)(2,1)}) fusion(bf16[16,4,128,2,2,64]{2,1,5,4,3,0:T(4,128)(2,1)} %reshape_squeeze.3), kind=kLoop, calls=%fused_computation.163 | loop fusion | bytes 8388608 | tf_op jit(solution)/shard_map/slice | solution.py:143
  66.4 0.6 fusion.31
  67.1 1.0 fusion.80
  68.2 0.2 copy.284
  68.4 0.3 fusion.45
  69.1 0.7 fusion.58
  69.7 0.2 copy.288
  70.1 0.1 copy.304
  70.2 0.6 reduce-window.6
  70.8 0.2 slice_reduce_fusion
  71.1 0.1 select_reduce_fusion.3
  71.2 0.1 reduce_or.9
  71.5 0.2 fusion.65
  71.7 64.2 %all-to-all-done = bf16[64,1,128,2,128]{4,3,2,1,0:T(2,128)(2,1)} async-done(((bf16[64,1,128,2,128]{4,3,2,1,0:T(2,128)(2,1)}), bf16[64,1,128,2,128]{4,3,2,1,0:T(2,128)(2,1)}, u32[]{:S(2)}, u32[]{:S(2)}) %all-to-all-start) | async-done | bytes 4194336 | tf_op jit(solution)/shard_map/all_to_all | solution.py:113
  135.8 10.9 %copy.272 = bf16[64,1,128,2,128]{2,4,3,0,1:T(8,128)(2,1)} copy(bf16[64,1,128,2,128]{4,3,2,1,0:T(2,128)(2,1)} %all-to-all-done) | data formatting | bytes 8388608 | tf_op jit(solution)/shard_map/all_to_all | solution.py:113
  146.8 3.1 fusion.6
  149.8 3.3 fusion.7
  153.1 0.1 copy.294
  153.2 0.3 multiply_reduce_fusion
  153.5 0.2 multiply_reduce_fusion.1
  153.8 11.1 %copy.345 = bf16[64,1,128,2,128]{2,4,0,3,1:T(8,128)(2,1)} copy(bf16[64,1,128,2,128]{4,3,2,1,0:T(2,128)(2,1)} %all-to-all-done) | data formatting | bytes 8388608 | tf_op jit(solution)/shard_map/reshape | solution.py:122
  165.0 3.0 fusion
  168.0 1.3 fusion.24
  169.3 0.1 fusion.44
  169.5 0.2 fusion.87
  169.7 1.6 collective-permute-start
  171.4 3.3 collective-permute-done
  174.8 3.5 collective-permute-start.1
  178.3 3.2 collective-permute-done.1
  181.5 0.1 fusion.37
  181.7 0.2 fusion.61
  181.9 0.2 select_reduce_fusion.1
  182.2 0.1 reduce_max.59
  182.4 0.6 convert_reduce_fusion
  183.0 1.8 convolution_convert_fusion
  184.7 2.4 reshape.522
  187.2 57.3 %all_to_all.15 = bf16[64,1,12,1024]{3,2,1,0:T(8,128)(2,1)S(1)} all-to-all(bf16[64,1,12,1024]{3,2,1,0:T(8,128)(2,1)S(1)} %bitcast.214), channel_id=1, replica_groups=mesh['req'=64,'tp'=4] {'req'}, dimensions={0} | all-to-all | bytes 3145728 | tf_op jit(solution)/shard_map/all_to_all | solution.py:221
  244.4 1.8 fusion.17
  246.2 0.6 fusion.16
  246.8 0.9 copy.321
  247.7 56.7 %all_to_all.16 = bf16[64,1,12,1024]{3,2,1,0:T(8,128)(2,1)} all-to-all(bf16[64,1,12,1024]{3,2,1,0:T(8,128)(2,1)S(1)} %copy.321), channel_id=1, replica_groups=mesh['req'=64,'tp'=4] {'req'}, dimensions={0} | all-to-all | bytes 3145728 | tf_op jit(solution)/shard_map/all_to_all | solution.py:227
  304.5 3.6 reshape.526
  308.1 2.9 convolution_convert_fusion.2
  311.0 43.0 %all-reduce.2.cloned.1.call-done = bf16[32,1024]{1,0:T(8,128)(2,1)} async-done(((bf16[32,1024]{1,0:T(8,128)(2,1)}), bf16[32,1024]{1,0:T(8,128)(2,1)}) %all-reduce.2.cloned.1.call-update) | async-done | bytes 65552 | tf_op jit(solution)/shard_map/psum | solution.py:231
  354.0 1.0 fusion.33
  355.0 0.7 reshape.527
  355.6 0.2 fusion.36
  355.9 0.7 copy.322
  (91 shorter events, 2.6 us)
Async XLA Ops:
  7.2 1.6 copy-start
  27.4 12.6 %copy-start.10 = (s32[1,16,2,8]{1,3,2,0:T(8,128)S(1)}, s32[1,16,2,8]{1,3,2,0:T(8,128)}, u32[]{:S(2)}) copy-start(s32[1,16,2,8]{1,3,2,0:T(8,128)} %param.23) | copy-start | bytes 3076
  27.4 12.9 %copy-start.16 = (s32[64]{0:T(128)S(1)}, s32[64]{0:T(128)}, u32[]{:S(2)}) copy-start(s32[64]{0:T(128)} %param.17) | copy-start | bytes 772
  27.4 13.5 %copy-start.4 = (bf16[1024,256]{1,0:T(8,128)(2,1)S(1)}, bf16[1024,256]{1,0:T(8,128)(2,1)}, u32[]{:S(2)}) copy-start(bf16[1024,256]{1,0:T(8,128)(2,1)} %param.25) | copy-start | bytes 1572868
  27.4 13.9 %copy-start.8 = (s32[2048]{0:T(1024)S(1)}, s32[2048]{0:T(1024)}, u32[]{:S(2)}) copy-start(s32[2048]{0:T(1024)} %param.19) | copy-start | bytes 24580
  27.4 14.0 %copy-start.11 = (s32[2048]{0:T(1024)S(1)}, s32[2048]{0:T(1024)}, u32[]{:S(2)}) copy-start(s32[2048]{0:T(1024)} %param.20) | copy-start | bytes 24580
  27.4 108.5 %all-to-all-start = ((bf16[64,1,128,2,128]{4,3,2,1,0:T(2,128)(2,1)}), bf16[64,1,128,2,128]{4,3,2,1,0:T(2,128)(2,1)}, u32[]{:S(2)}, u32[]{:S(2)}) async-start(bf16[64,1,128,2,128]{4,3,2,1,0:T(2,128)(2,1)} %fusion.4), calls=%async_computation | async-start | bytes 8388608 | tf_op jit(solution)/shard_map/all_to_all | solution.py:113
  39.7 314.3 %all-reduce.2.cloned.1.call-start = ((), (), s32[]{:S(2)}) async-start(), calls=%async_computation.3 | async-start | bytes 131072 | tf_op jit(solution)/shard_map/psum | solution.py:231
  52.6 7.0 %copy-start.3 = (bf16[1,16,2,1024]{3,2,1,0:T(2,128)(2,1)S(1)}, bf16[1,16,2,1024]{3,2,1,0:T(2,128)(2,1)}, u32[]{:S(2)}) copy-start(bf16[1,16,2,1024]{3,2,1,0:T(2,128)(2,1)} %param.16) | copy-start | bytes 196612
  52.6 7.8 %copy-start.13 = (s32[1,16]{1,0:T(1,128)S(1)}, s32[1,16]{1,0:T(1,128)}, u32[]{:S(2)}) copy-start(s32[1,16]{1,0:T(1,128)} %param.18) | copy-start | bytes 196
  52.6 7.8 %copy-start.9 = (f32[3,1024]{1,0:T(4,128)S(1)}, f32[3,1024]{1,0:T(4,128)}, u32[]{:S(2)}) copy-start(f32[3,1024]{1,0:T(4,128)} %param.24) | copy-start | bytes 36868
  66.4 1.7 copy-start.5
  165.0 3.0 copy-start.2
  168.0 1.6 copy-start.6
  168.0 13.7 %copy-start.15 = (bf16[1024,32]{0,1:T(8,128)(2,1)S(1)}, bf16[1024,32]{0,1:T(8,128)(2,1)}, u32[]{:S(2)}) copy-start(bf16[1024,32]{0,1:T(8,128)(2,1)} %param.28) | copy-start | bytes 196612
  169.7 5.0 %collective-permute-start = (f32[32,1024]{1,0:T(8,128)S(1)}, f32[32,1024]{1,0:T(8,128)S(1)}, u32[]{:S(2)}, u32[]{:S(2)}) collective-permute-start(f32[32,1024]{1,0:T(8,128)S(1)} %fusion.87), channel_id=1, source_target_pairs={{0,1},{1,0},{2,3},{3,2},{4,5},{5,4},{6,7},{7,6},{8,9},{9,8},{10,11... | collective-permute-start | bytes 393224 | tf_op jit(solution)/shard_map/ppermute | solution.py:191
  174.8 6.8 %collective-permute-start.1 = (f32[32,1024]{1,0:T(8,128)S(1)}, f32[32,1024]{1,0:T(8,128)S(1)}, u32[]{:S(2)}, u32[]{:S(2)}) collective-permute-start(f32[32,1024]{1,0:T(8,128)S(1)} %add.198), channel_id=1, source_target_pairs={{0,2},{1,3},{2,0},{3,1},{4,6},{5,7},{6,4},{7,5},{8,10},{9,11},{10,... | collective-permute-start | bytes 393224 | tf_op jit(solution)/shard_map/ppermute | solution.py:191
  184.7 59.7 %copy-start.14 = (bf16[1,1024,2,128]{3,2,1,0:T(2,128)(2,1)S(1)}, bf16[1,1024,2,128]{3,2,1,0:T(2,128)(2,1)}, u32[]{:S(2)}) copy-start(bf16[1,1024,2,128]{3,2,1,0:T(2,128)(2,1)} %param.29) | copy-start | bytes 1572868
  187.2 59.1 %copy-start.7 = (bf16[1,128,1024]{2,1,0:T(8,128)(2,1)S(1)}, bf16[1,128,1024]{2,1,0:T(8,128)(2,1)}, u32[]{:S(2)}) copy-start(bf16[1,128,1024]{2,1,0:T(8,128)(2,1)} %param.30) | copy-start | bytes 786436
  247.7 108.8 %copy-start.1 = (bf16[32,128,2,128]{3,2,1,0:T(2,128)(2,1)S(1)}, bf16[32,128,2,128]{3,2,1,0:T(2,128)(2,1)}, u32[]{:S(2)}) copy-start(bf16[32,128,2,128]{3,2,1,0:T(2,128)(2,1)} %param.21) | copy-start | bytes 6291460
  304.5 51.2 %copy-start.12 = (f32[1024]{0:T(1024)S(1)}, f32[1024]{0:T(1024)}, u32[]{:S(2)}) copy-start(f32[1024]{0:T(1024)} %param.31) | copy-start | bytes 12292
Sparse Core Ops, SparseCore 0:
  311.1 42.7 all-reduce.1
